TPU v7x, 32 devices: a whole 2x2x4 slice. The times are simulated.
32 devices in a mesh: energy: 8 (over z, y), cell: 4 (over x, core).
Axes of the slice: x: 2, y: 2, z: 4, core: 2. Of those that a mesh axis runs over, the one named last changes fastest.
Arguments:
- retarded: bfloat16 [4, 2, 32, 256, 256], P('cell', None, 'energy'), may hold values from -0.25 to 0.25
- sigma_lesser: bfloat16 [4, 2, 32, 256, 256], P('cell', None, 'energy'), may hold values from -6 to 6
- sigma_greater: bfloat16 [4, 2, 32, 256, 256], P('cell', None, 'energy'), may hold values from -6 to 6
- coulomb: bfloat16 [4, 3, 256, 256], P('cell'), may hold values from -0.21875 to 0.21875
Outputs:
- screened: bfloat16 [4, 2, 32, 256, 256], P('cell', None, 'energy')
All inputs are finite; a program needn't handle non-finite values.
Results may differ from a plain program's by a relative error of at most 0.009.
Values may be sent and summed in bfloat16 or wider, within the bound.
A program may use at most 64 MiB of HBM per device.

v0:
```python
import math

import jax
import jax.numpy as jnp
from jax import lax
from jax.sharding import PartitionSpec as P


def with_halo(block, sides, width):
    for axis, dim in sides:
        count = lax.axis_size(axis)
        forward = [(i, i + 1) for i in range(count - 1)]
        backward = [(target, source) for source, target in forward]
        low = lax.ppermute(
            lax.slice_in_dim(block, block.shape[dim] - width, None, axis=dim), axis, forward
        )
        high = lax.ppermute(lax.slice_in_dim(block, 0, width, axis=dim), axis, backward)
        block = jnp.concatenate([low, block, high], axis=dim)
    return block


def complex_product(first_re, first_im, second_re, second_im):
    real_part = jnp.einsum(
        "eik,ekj->eij", first_re, second_re, preferred_element_type=jnp.float32
    ) - jnp.einsum("eik,ekj->eij", first_im, second_im, preferred_element_type=jnp.float32)
    imag_part = jnp.einsum(
        "eik,ekj->eij", first_re, second_im, preferred_element_type=jnp.float32
    ) + jnp.einsum("eik,ekj->eij", first_im, second_re, preferred_element_type=jnp.float32)
    return (real_part.astype(jnp.bfloat16), imag_part.astype(jnp.bfloat16))


def adjoint_product(first_re, first_im, green_re, green_im):
    real_part = jnp.einsum(
        "eik,ejk->eij", first_re, green_re, preferred_element_type=jnp.float32
    ) + jnp.einsum("eik,ejk->eij", first_im, green_im, preferred_element_type=jnp.float32)
    imag_part = jnp.einsum(
        "eik,ejk->eij", first_im, green_re, preferred_element_type=jnp.float32
    ) - jnp.einsum("eik,ejk->eij", first_re, green_im, preferred_element_type=jnp.float32)
    return jnp.stack([real_part, imag_part]).astype(jnp.bfloat16)


def triple(green, sigma):
    half_re, half_im = complex_product(green[0], green[1], sigma[0], sigma[1])
    return adjoint_product(half_re, half_im, green[0], green[1])


def tables(energies):
    length = 2 * energies
    frequency = lax.broadcasted_iota(jnp.int32, (length, energies), 0)
    energy_index = lax.broadcasted_iota(jnp.int32, (length, energies), 1)
    angles = 2.0 * math.pi / length * (frequency * energy_index % length).astype(jnp.float32)
    cos_table = jnp.cos(angles)
    sin_table = jnp.sin(angles)
    forward_first = jnp.concatenate(
        [jnp.concatenate([cos_table, sin_table], 1), jnp.concatenate([-sin_table, cos_table], 1)], 0
    )
    forward_second = jnp.concatenate(
        [jnp.concatenate([cos_table, -sin_table], 1), jnp.concatenate([sin_table, cos_table], 1)], 0
    )
    factor = 1.0 / (length * math.sqrt(energies))
    inverse = (
        jnp.concatenate(
            [
                jnp.concatenate([cos_table.T, -sin_table.T], 1),
                jnp.concatenate([sin_table.T, cos_table.T], 1),
            ],
            0,
        )
        * factor
    )
    return (
        forward_first.astype(jnp.bfloat16),
        forward_second.astype(jnp.bfloat16),
        inverse.astype(jnp.bfloat16),
    )


def correlate(lesser, mirrored):
    energies = lesser.shape[1]
    length = 2 * energies
    elements = lesser.shape[2] * lesser.shape[3]
    forward_first, forward_second, inverse = tables(energies)
    first_flat = lesser.reshape(2 * energies, elements)
    second_flat = mirrored.reshape(2 * energies, elements)
    spec_first = jnp.dot(forward_first, first_flat, preferred_element_type=jnp.float32)
    spec_second = jnp.dot(forward_second, second_flat, preferred_element_type=jnp.float32)
    left_re, left_im = (spec_first[:length], spec_first[length:])
    right_re, right_im = (spec_second[:length], spec_second[length:])
    product = jnp.concatenate(
        [left_re * right_re - left_im * right_im, left_re * right_im + left_im * right_re], 0
    ).astype(jnp.bfloat16)
    lag_values = jnp.dot(inverse, product, preferred_element_type=jnp.float32)
    return lag_values.reshape(lesser.shape).astype(jnp.bfloat16)


def return_lags(polarized):
    return lax.all_to_all(polarized, "energy", split_axis=1, concat_axis=2, tiled=True)


def on_device(retarded, sigma_lesser, sigma_greater, coulomb):
    lesser = triple(retarded[0], sigma_lesser[0])
    greater = triple(retarded[0], sigma_greater[0])
    lesser_strip = lax.all_to_all(lesser, "energy", split_axis=2, concat_axis=1, tiled=True)
    greater_strip = lax.all_to_all(greater, "energy", split_axis=3, concat_axis=1, tiled=True)
    polarized = return_lags(correlate(lesser_strip, jnp.swapaxes(greater_strip, 2, 3)))
    coulomb_rows = coulomb[0]
    expanded = polarized[None]
    padded = with_halo(expanded, (("cell", 0),), 1)
    summed = jnp.einsum("dik,dcekj->ceij", coulomb_rows, padded, preferred_element_type=jnp.float32)
    return summed.astype(jnp.bfloat16)[None]


def solution(mesh):
    in_specs = (
        P("cell", None, "energy", None, None),
        P("cell", None, "energy", None, None),
        P("cell", None, "energy", None, None),
        P("cell", None, None, None),
    )
    out_specs = P("cell", None, "energy", None, None)
    return jax.shard_map(
        on_device, mesh=mesh, in_specs=in_specs, out_specs=out_specs, check_vma=False
    )
```

profile of v0, /device:TPU:1, one launch (start us, length us, event | category | flops | bytes accessed | tf_op | source)
XLA Modules:
  0.0 124.3 jit_solution(15394455906207490821)
XLA Ops:
  0.0 1.6 %fusion.32 = f32[4,256,256]{2,1,0:T(8,128)S(1)} fusion(bf16[1,2,4,256,256]{4,3,2,1,0:T(8,128)(2,1)} %param.5, bf16[1,2,4,256,256]{4,3,2,1,0:T(8,128)(2,1)} %param.4), kind=kOutput, calls=%fused_computation.42 | convolution fusion | flops 134217728 | bytes 2097152 | tf_op jit(solution)/shard_map/eik,ekj->eij/dot_general | solution.py:26
  4.3 1.8 %copy.22 = bf16[2,4,256,256]{3,1,0,2:T(4,128)(2,1)} copy(bf16[2,4,256,256]{3,2,1,0:T(8,128)(2,1)S(1)} %pad_maximum_fusion) | data formatting | bytes 2097152 | tf_op jit(solution)/shard_map/stack | solution.py:39
  6.1 6.4 %all-to-all-start = ((bf16[2,4,256,256]{3,1,0,2:T(4,128)(2,1)}), bf16[2,4,256,256]{3,1,0,2:T(4,128)(2,1)S(1)}, u32[]{:S(2)}, u32[]{:S(2)}) async-start(bf16[2,4,256,256]{3,1,0,2:T(4,128)(2,1)} %copy.22), calls=%async_computation | async-start | bytes 2097152 | tf_op jit(solution)/shard_map/all_to_all | solution.py:103
  15.2 1.8 %copy.24 = bf16[2,4,256,256]{2,1,0,3:T(4,128)(2,1)} copy(bf16[2,4,256,256]{3,2,1,0:T(8,128)(2,1)S(1)} %pad_maximum_fusion.1) | data formatting | bytes 2097152 | tf_op jit(solution)/shard_map/stack | solution.py:39
  17.0 20.5 %all-to-all-done = bf16[2,4,256,256]{3,1,0,2:T(4,128)(2,1)S(1)} async-done(((bf16[2,4,256,256]{3,1,0,2:T(4,128)(2,1)}), bf16[2,4,256,256]{3,1,0,2:T(4,128)(2,1)S(1)}, u32[]{:S(2)}, u32[]{:S(2)}) %all-to-all-start) | async-done | bytes 1048608 | tf_op jit(solution)/shard_map/all_to_all | solution.py:103
  37.4 4.6 %all-to-all-start.1 = ((bf16[2,4,256,256]{2,1,0,3:T(4,128)(2,1)}), bf16[2,4,256,256]{2,1,0,3:T(4,128)(2,1)S(1)}, u32[]{:S(2)}, u32[]{:S(2)}) async-start(bf16[2,4,256,256]{2,1,0,3:T(4,128)(2,1)} %copy.24), calls=%async_computation.1 | async-start | bytes 2097152 | tf_op jit(solution)/shard_map/all_to_all | solution.py:104
  42.2 0.7 fusion.112
  42.9 0.8 negate_convert_fusion
  43.6 0.7 fusion.110
  44.6 0.6 copy.37
  45.2 21.9 %all-to-all-done.1 = bf16[2,4,256,256]{2,1,0,3:T(4,128)(2,1)S(1)} async-done(((bf16[2,4,256,256]{2,1,0,3:T(4,128)(2,1)}), bf16[2,4,256,256]{2,1,0,3:T(4,128)(2,1)S(1)}, u32[]{:S(2)}, u32[]{:S(2)}) %all-to-all-start.1) | async-done | bytes 1048608 | tf_op jit(solution)/shard_map/all_to_all | solution.py:104
  67.5 0.6 copy.38
  68.1 0.8 fusion.84
  68.9 0.8 fusion.87
  69.7 0.6 subtract_convert_fusion
  70.4 0.5 convolution_convert_fusion
  71.2 29.0 %all_to_all.48 = bf16[2,32,32,256]{3,2,0,1:T(8,128)(2,1)S(1)} all-to-all(bf16[2,32,32,256]{3,2,0,1:T(8,128)(2,1)S(1)} %copy.27), channel_id=1, replica_groups=mesh['energy'=8,'cell'=4] {'energy'}, dimensions={1} | all-to-all | bytes 2097152 | tf_op jit(solution)/shard_map/all_to_all | solution.py:97
  100.3 0.5 copy.30
  100.9 4.9 %collective-permute-start = (bf16[1,2,4,256,256]{3,4,0,2,1:T(8,128)(2,1)S(1)}, bf16[1,2,4,256,256]{3,4,0,2,1:T(8,128)(2,1)S(1)}, u32[]{:S(2)}, u32[]{:S(2)}) collective-permute-start(bf16[1,2,4,256,256]{3,4,0,2,1:T(8,128)(2,1)S(1)} %copy.30), channel_id=1, source_target_pairs={{0,1},{1,2},{2,3},{4,5},{5,6},{6,7},{8,9},{9,10},{10,11},{12,13},{... | collective-permute-start | bytes 3145736 | tf_op jit(solution)/shard_map/ppermute | solution.py:14
  105.8 1.9 %collective-permute-start.1 = (bf16[1,2,4,256,256]{3,4,0,2,1:T(8,128)(2,1)S(1)}, bf16[1,2,4,256,256]{3,4,0,2,1:T(8,128)(2,1)S(1)}, u32[]{:S(2)}, u32[]{:S(2)}) collective-permute-start(bf16[1,2,4,256,256]{3,4,0,2,1:T(8,128)(2,1)S(1)} %copy.30), channel_id=1, source_target_pairs={{1,0},{2,1},{3,2},{5,4},{6,5},{7,6},{9,8},{10,9},{11,10},{13,12},{... | collective-permute-start | bytes 3145736 | tf_op jit(solution)/shard_map/ppermute | solution.py:17
  107.8 9.8 %collective-permute-done = bf16[1,2,4,256,256]{3,4,0,2,1:T(8,128)(2,1)S(1)} collective-permute-done((bf16[1,2,4,256,256]{3,4,0,2,1:T(8,128)(2,1)S(1)}, bf16[1,2,4,256,256]{3,4,0,2,1:T(8,128)(2,1)S(1)}, u32[]{:S(2)}, u32[]{:S(2)}) %collective-permute-start) | collective-permute-done | bytes 1048608 | tf_op jit(solution)/shard_map/ppermute | solution.py:14
  117.5 4.4 %collective-permute-done.1 = bf16[1,2,4,256,256]{3,4,0,2,1:T(8,128)(2,1)S(1)} collective-permute-done((bf16[1,2,4,256,256]{3,4,0,2,1:T(8,128)(2,1)S(1)}, bf16[1,2,4,256,256]{3,4,0,2,1:T(8,128)(2,1)S(1)}, u32[]{:S(2)}, u32[]{:S(2)}) %collective-permute-start.1) | collective-permute-done | bytes 1048608 | tf_op jit(solution)/shard_map/ppermute | solution.py:17
  121.9 1.0 fusion.11
  123.0 1.3 %copy.33 = bf16[1,2,4,256,256]{4,3,2,1,0:T(8,128)(2,1)} copy(bf16[1,2,4,256,256]{3,4,2,1,0:T(8,128)(2,1)S(1)} %fusion.11) | data formatting | bytes 2097152 | tf_op jit(solution)/shard_map/broadcast_in_dim | solution.py:110
  (42 shorter events, 6.5 us)
Async XLA Ops:
  0.0 121.9 %copy-start = (bf16[1,3,256,256]{3,2,1,0:T(8,128)(2,1)S(1)}, bf16[1,3,256,256]{3,2,1,0:T(8,128)(2,1)}, u32[]{:S(2)}) copy-start(bf16[1,3,256,256]{3,2,1,0:T(8,128)(2,1)} %param.7) | copy-start | bytes 1179652
  0.0 1.7 %copy-start.1 = (bf16[1,2,4,256,256]{4,3,2,1,0:T(8,128)(2,1)S(1)}, bf16[1,2,4,256,256]{4,3,2,1,0:T(8,128)(2,1)}, u32[]{:S(2)}) copy-start(bf16[1,2,4,256,256]{4,3,2,1,0:T(8,128)(2,1)} %param.4) | copy-start | bytes 3145732
  0.0 1.9 %copy-start.2 = (bf16[1,2,4,256,256]{4,3,2,1,0:T(8,128)(2,1)S(1)}, bf16[1,2,4,256,256]{4,3,2,1,0:T(8,128)(2,1)}, u32[]{:S(2)}) copy-start(bf16[1,2,4,256,256]{4,3,2,1,0:T(8,128)(2,1)} %param.5) | copy-start | bytes 3145732
  4.3 8.2 %copy-start.3 = (bf16[1,2,4,256,256]{4,3,2,1,0:T(8,128)(2,1)S(1)}, bf16[1,2,4,256,256]{4,3,2,1,0:T(8,128)(2,1)}, u32[]{:S(2)}) copy-start(bf16[1,2,4,256,256]{4,3,2,1,0:T(8,128)(2,1)} %param.6) | copy-start | bytes 3145732
  6.1 31.3 %all-to-all-start = ((bf16[2,4,256,256]{3,1,0,2:T(4,128)(2,1)}), bf16[2,4,256,256]{3,1,0,2:T(4,128)(2,1)S(1)}, u32[]{:S(2)}, u32[]{:S(2)}) async-start(bf16[2,4,256,256]{3,1,0,2:T(4,128)(2,1)} %copy.22), calls=%async_computation | async-start | bytes 2097152 | tf_op jit(solution)/shard_map/all_to_all | solution.py:103
  37.4 29.7 %all-to-all-start.1 = ((bf16[2,4,256,256]{2,1,0,3:T(4,128)(2,1)}), bf16[2,4,256,256]{2,1,0,3:T(4,128)(2,1)S(1)}, u32[]{:S(2)}, u32[]{:S(2)}) async-start(bf16[2,4,256,256]{2,1,0,3:T(4,128)(2,1)} %copy.24), calls=%async_computation.1 | async-start | bytes 2097152 | tf_op jit(solution)/shard_map/all_to_all | solution.py:104
  67.4 0.7 copy-start.4
  67.4 0.7 copy-start.5
  69.6 0.7 copy-start.6
  69.7 0.7 copy-start.7
  69.7 0.7 copy-start.8
  100.9 16.7 %collective-permute-start = (bf16[1,2,4,256,256]{3,4,0,2,1:T(8,128)(2,1)S(1)}, bf16[1,2,4,256,256]{3,4,0,2,1:T(8,128)(2,1)S(1)}, u32[]{:S(2)}, u32[]{:S(2)}) collective-permute-start(bf16[1,2,4,256,256]{3,4,0,2,1:T(8,128)(2,1)S(1)} %copy.30), channel_id=1, source_target_pairs={{0,1},{1,2},{2,3},{4,5},{5,6},{6,7},{8,9},{9,10},{10,11},{12,13},{... | collective-permute-start | bytes 3145736 | tf_op jit(solution)/shard_map/ppermute | solution.py:14
  105.8 16.1 %collective-permute-start.1 = (bf16[1,2,4,256,256]{3,4,0,2,1:T(8,128)(2,1)S(1)}, bf16[1,2,4,256,256]{3,4,0,2,1:T(8,128)(2,1)S(1)}, u32[]{:S(2)}, u32[]{:S(2)}) collective-permute-start(bf16[1,2,4,256,256]{3,4,0,2,1:T(8,128)(2,1)S(1)} %copy.30), channel_id=1, source_target_pairs={{1,0},{2,1},{3,2},{5,4},{6,5},{7,6},{9,8},{10,9},{11,10},{13,12},{... | collective-permute-start | bytes 3145736 | tf_op jit(solution)/shard_map/ppermute | solution.py:17
where the time goes:
time: 125 us; the launch traced here: 124 us
  waiting for transfers between devices  56.6 us (45%)
  blocking collectives  29 us (23%)
  starting transfers between devices  17.8 us (14%)
  matrix products  9.44 us (8%)
  local copies, waits for them, and re-layouts  8.04 us (6%)
  other arithmetic  3.08 us (2%)
    all_to_all x1, blocking collectives, return_lags(): lax.all_to_all(polarized, 'energy', split_axis=1, concat_axis=2, tiled=True)  29 us
    all_to_all x1, waiting for transfers between devices, on_device(): lax.all_to_all(greater, 'energy', split_axis=3, concat_axis=1, tiled=True)  21.9 us
    all_to_all x1, waiting for transfers between devices, on_device(): lax.all_to_all(lesser, 'energy', split_axis=2, concat_axis=1, tiled=True)  20.5 us
    ppermute x1, waiting for transfers between devices, with_halo(): lax.ppermute(lax.slice_in_dim(block, block.shape[dim] - width, None, axis...  9.79 us
    all_to_all x1, starting transfers between devices, on_device(): lax.all_to_all(lesser, 'energy', split_axis=2, concat_axis=1, tiled=True)  6.37 us
    ppermute x1, starting transfers between devices, with_halo(): lax.ppermute(lax.slice_in_dim(block, block.shape[dim] - width, None, axis...  4.93 us
    all_to_all x1, starting transfers between devices, on_device(): lax.all_to_all(greater, 'energy', split_axis=3, concat_axis=1, tiled=True)  4.58 us
    ppermute x1, waiting for transfers between devices, with_halo(): lax.ppermute(lax.slice_in_dim(block, 0, width, axis=dim), axis, backward)  4.4 us
  transfers between devices with their start and end apart: 4, of which 4 were waited for; matrix products, arithmetic and copies ran while one was open for 6% of the time, Pallas kernels for 0%

commit v1 on v0

v1 whole, which is shorter than its diff:
```python
import functools
import math

import jax
import jax.numpy as jnp
from jax import lax
from jax.experimental import pallas as pl
from jax.experimental.pallas import tpu as pltpu
from jax.sharding import PartitionSpec as P

MESH = pl.DeviceIdType.MESH
ROWS = 16
LANES = 128
F32 = jnp.float32
BF16 = jnp.bfloat16


def nn(a, b):
    return jnp.dot(a, b, preferred_element_type=F32)


def nt(a, b):
    return lax.dot_general(a, b, (((1,), (1,)), ((), ())), preferred_element_type=F32)


def fused_kernel(
    n, cells, green, sig_l, sig_g, coulomb, out,
    send, recv, send_p, pol, total,
    send_sem, recv_sem, ret_send_sem, ret_recv_sem, halo_send_sem, halo_recv_sem,
):
    me = lax.axis_index("energy")
    cell = lax.axis_index("cell")
    local = green.shape[1]
    norb = green.shape[2]
    strip = norb // n
    row_parts, col_parts = strip // ROWS, norb // LANES
    chunks = row_parts * col_parts
    has_low = cell > 0
    has_high = cell < cells - 1

    barrier = pltpu.get_barrier_semaphore()

    @pl.loop(1, n)
    def _(k):
        pl.semaphore_signal(barrier, inc=1, device_id={"energy": lax.rem(me + k, n)}, device_id_type=MESH)

    @pl.when(has_low)
    def _():
        pl.semaphore_signal(barrier, inc=1, device_id={"cell": cell - 1}, device_id_type=MESH)

    @pl.when(has_high)
    def _():
        pl.semaphore_signal(barrier, inc=1, device_id={"cell": cell + 1}, device_id_type=MESH)

    def put(value, comp, e):
        value = value.astype(BF16).reshape(n, strip, norb)
        for q in range(chunks):
            r, c = divmod(q, col_parts)
            send[q, :, comp, e] = value[:, r * ROWS:(r + 1) * ROWS, c * LANES:(c + 1) * LANES]

    @pl.loop(0, local)
    def _(e):
        g_re, g_im = green[0, e], green[1, e]
        l_re, l_im = sig_l[0, e], sig_l[1, e]
        half_re = (nn(g_re, l_re) - nn(g_im, l_im)).astype(BF16)
        half_im = (nn(g_re, l_im) + nn(g_im, l_re)).astype(BF16)
        put(nt(half_re, g_re) + nt(half_im, g_im), 0, e)
        put(nt(half_im, g_re) - nt(half_re, g_im), 1, e)
        s_re, s_im = sig_g[0, e], sig_g[1, e]
        half_re = (nn(g_re, s_re) - nn(g_im, s_im)).astype(BF16)
        half_im = (nn(g_re, s_im) + nn(g_im, s_re)).astype(BF16)
        put(nt(g_re, half_re) + nt(g_im, half_im), 2, e)
        put(nt(g_re, half_im) - nt(g_im, half_re), 3, e)

    pl.semaphore_wait(barrier, n - 1 + has_low.astype(jnp.int32) + has_high.astype(jnp.int32))

    def strip_copy(q, slot, peer):
        return pltpu.make_async_remote_copy(
            src_ref=send.at[q, peer], dst_ref=recv.at[q, slot],
            send_sem=send_sem.at[q, peer], recv_sem=recv_sem.at[q, slot],
            device_id={"energy": peer}, device_id_type=MESH,
        )

    @pl.loop(0, chunks)
    def _(q):
        @pl.loop(1, n)
        def _(k):
            strip_copy(q, me, lax.rem(me + k, n)).start()

    @pl.loop(0, chunks)
    def _(q):
        recv[q, me] = send[q, me]
        recv[q, n] = jnp.zeros_like(recv[q, n])

    @pl.when(jnp.logical_not(has_low))
    def _():
        pol[0] = jnp.zeros_like(pol[0])

    @pl.when(jnp.logical_not(has_high))
    def _():
        pol[2] = jnp.zeros_like(pol[2])

    def window(slot, owner, q):
        rows = pl.ds(pl.multiple_of(q // col_parts * ROWS, ROWS), ROWS)
        cols = pl.ds(pl.multiple_of(q % col_parts * LANES, LANES), LANES)
        return pol.at[slot, :, :, owner, rows, cols]

    def return_copy(q, slot, peer):
        return pltpu.make_async_remote_copy(
            src_ref=send_p.at[q, peer], dst_ref=window(1, slot, q),
            send_sem=ret_send_sem.at[q, peer], recv_sem=ret_recv_sem.at[q, slot],
            device_id={"energy": peer}, device_id_type=MESH,
        )

    factor = 1.0 / math.sqrt(n * local)

    def correlate(q, b):
        def step(a, acc):
            first = [
                (recv[q, a + b + i // local, 0, i % local].astype(F32), recv[q, a + b + i // local, 1, i % local].astype(F32))
                for i in range(2 * local - 1)
            ]
            acc = list(acc)
            for e in range(local):
                x_re, x_im = recv[q, a, 2, e].astype(F32), recv[q, a, 3, e].astype(F32)
                for w in range(local):
                    y_re, y_im = first[e + w]
                    acc[2 * w] = acc[2 * w] + (y_re * x_re - y_im * x_im)
                    acc[2 * w + 1] = acc[2 * w + 1] + (y_re * x_im + y_im * x_re)
            return tuple(acc)

        zero = jnp.zeros((ROWS, LANES), F32)
        acc = lax.fori_loop(0, n - b, step, (zero,) * (2 * local))
        for w in range(local):
            send_p[q, b, 0, w] = (acc[2 * w] * factor).astype(BF16)
            send_p[q, b, 1, w] = (acc[2 * w + 1] * factor).astype(BF16)

    @pl.loop(0, chunks)
    def _(q):
        @pl.loop(1, n)
        def _(k):
            strip_copy(q, lax.rem(me + k, n), lax.rem(me + k, n)).wait_recv()

        @pl.loop(1, n)
        def _(k):
            peer = lax.rem(me + k, n)
            correlate(q, peer)
            return_copy(q, me, peer).start()

        correlate(q, me)
        window(1, me, q)[...] = send_p[q, me]

    def halo_copy(q, slot, other):
        rows = pl.ds(pl.multiple_of(q // col_parts * ROWS, ROWS), ROWS)
        cols = pl.ds(pl.multiple_of(q % col_parts * LANES, LANES), LANES)
        return pltpu.make_async_remote_copy(
            src_ref=pol.at[1, :, :, :, rows, cols], dst_ref=pol.at[slot, :, :, :, rows, cols],
            send_sem=halo_send_sem.at[q, slot // 2], recv_sem=halo_recv_sem.at[q, slot // 2],
            device_id={"cell": other}, device_id_type=MESH,
        )

    @pl.loop(0, chunks)
    def _(q):
        @pl.loop(1, n)
        def _(k):
            return_copy(q, lax.rem(me + k, n), lax.rem(me + k, n)).wait_recv()

        @pl.when(has_low)
        def _():
            halo_copy(q, 2, cell - 1).start()

        @pl.when(has_high)
        def _():
            halo_copy(q, 0, cell + 1).start()

    def polarized(slot, c, e):
        return pol[slot, c, e].reshape(norb, norb)

    @pl.loop(0, local)
    def _(e):
        for c in range(2):
            total[c, e] = nn(coulomb[1], polarized(1, c, e))

    @pl.loop(0, chunks)
    def _(q):
        @pl.when(has_low)
        def _():
            halo_copy(q, 0, cell - 1).wait_recv()
            halo_copy(q, 2, cell - 1).wait_send()

        @pl.when(has_high)
        def _():
            halo_copy(q, 2, cell + 1).wait_recv()
            halo_copy(q, 0, cell + 1).wait_send()

    @pl.loop(0, local)
    def _(e):
        for c in range(2):
            summed = total[c, e] + nn(coulomb[0], polarized(0, c, e)) + nn(coulomb[2], polarized(2, c, e))
            out[c, e] = summed.astype(BF16)

    @pl.loop(0, chunks)
    def _(q):
        @pl.loop(1, n)
        def _(k):
            peer = lax.rem(me + k, n)
            strip_copy(q, me, peer).wait_send()
            return_copy(q, me, peer).wait_send()


def fused(n, cells, retarded, sigma_lesser, sigma_greater, coulomb):
    green = retarded[0]
    local, norb = green.shape[1], green.shape[2]
    strip = norb // n
    chunks = strip // ROWS * (norb // LANES)
    vmem = pl.BlockSpec(memory_space=pltpu.VMEM)
    dma = pltpu.SemaphoreType.DMA
    result = pl.pallas_call(
        functools.partial(fused_kernel, n, cells),
        out_shape=jax.ShapeDtypeStruct(green.shape, BF16),
        in_specs=[vmem] * 4,
        out_specs=vmem,
        scratch_shapes=[
            pltpu.VMEM((chunks, n, 4, local, ROWS, LANES), BF16),
            pltpu.VMEM((chunks, n + 1, 4, local, ROWS, LANES), BF16),
            pltpu.VMEM((chunks, n, 2, local, ROWS, LANES), BF16),
            pltpu.VMEM((3, 2, local, n, strip, norb), BF16),
            pltpu.VMEM((2, local, norb, norb), F32),
            dma((chunks, n)), dma((chunks, n)), dma((chunks, n)), dma((chunks, n)),
            dma((chunks, 2)), dma((chunks, 2)),
        ],
        compiler_params=pltpu.CompilerParams(
            collective_id=0, has_side_effects=True, vmem_limit_bytes=48 * 1024 * 1024
        ),
    )(green, sigma_lesser[0], sigma_greater[0], coulomb[0])
    return result[None]


def thin(n, cells, retarded, sigma_lesser, sigma_greater, coulomb):
    green = retarded[0]
    local = green.shape[1]

    def halves(sigma):
        def product(x, y):
            return jnp.einsum("eik,ekj->eij", x, y, preferred_element_type=F32)

        re = product(green[0], sigma[0]) - product(green[1], sigma[1])
        im = product(green[0], sigma[1]) + product(green[1], sigma[0])
        return re.astype(BF16), im.astype(BF16)

    def adjoint(x, y):
        return jnp.einsum("eik,ejk->eij", x, y, preferred_element_type=F32)

    re, im = halves(sigma_lesser[0])
    lesser = jnp.stack([adjoint(re, green[0]) + adjoint(im, green[1]), adjoint(im, green[0]) - adjoint(re, green[1])])
    re, im = halves(sigma_greater[0])
    greater = jnp.stack([adjoint(green[0], re) + adjoint(green[1], im), adjoint(green[0], im) - adjoint(green[1], re)])
    first = lax.all_to_all(lesser.astype(BF16), "energy", split_axis=2, concat_axis=1, tiled=True).astype(F32)
    second = lax.all_to_all(greater.astype(BF16), "energy", split_axis=2, concat_axis=1, tiled=True).astype(F32)
    energies = n * local
    padded = jnp.concatenate([first, jnp.zeros_like(first)], axis=1)

    def lag(w):
        y = lax.dynamic_slice_in_dim(padded, w, energies, axis=1)
        re = jnp.sum(y[0] * second[0] - y[1] * second[1], axis=0)
        im = jnp.sum(y[0] * second[1] + y[1] * second[0], axis=0)
        return (jnp.stack([re, im]) / math.sqrt(energies)).astype(BF16)

    polarized = jnp.swapaxes(lax.map(lag, jnp.arange(energies)), 0, 1)
    polarized = lax.all_to_all(polarized, "energy", split_axis=1, concat_axis=2, tiled=True)
    up = [(i, i + 1) for i in range(cells - 1)]
    low = lax.ppermute(polarized, "cell", up)
    high = lax.ppermute(polarized, "cell", [(t, s) for s, t in up])
    stacked = jnp.stack([low, polarized, high])
    summed = jnp.einsum("dik,dcekj->ceij", coulomb[0], stacked, preferred_element_type=F32)
    return summed.astype(BF16)[None]


def solution(mesh):
    n, cells = mesh.shape["energy"], mesh.shape["cell"]

    def on_device(retarded, sigma_lesser, sigma_greater, coulomb):
        norb = retarded.shape[-1]
        whole_tiles = norb % LANES == 0 and norb % (n * ROWS) == 0
        plan = fused if whole_tiles else thin
        return plan(n, cells, retarded, sigma_lesser, sigma_greater, coulomb)

    in_specs = (
        P("cell", None, "energy", None, None),
        P("cell", None, "energy", None, None),
        P("cell", None, "energy", None, None),
        P("cell", None, None, None),
    )
    out_specs = P("cell", None, "energy", None, None)
    return jax.shard_map(
        on_device, mesh=mesh, in_specs=in_specs, out_specs=out_specs, check_vma=False
    )
```

time: 125 us -> 90.1 us (0.72)
  Pallas kernels: 0 us -> 84.2 us
  waiting for transfers between devices: 56.6 us -> 0 us
  blocking collectives: 29 us -> 0 us
  starting transfers between devices: 17.8 us -> 0 us
  matrix products: 9.44 us -> 0 us
  other arithmetic: 3.08 us -> 0 us
  local copies, waits for them, and re-layouts: 8.04 us -> 5.64 us
    pallas_call x0 -> x1, Pallas kernels: none -> 84.2 us  [fused(): pl.pallas_call(functools.partial(fused_kernel, n, cells), out_shape=jax.S...]
    all_to_all x2 -> x0, waiting for transfers between devices: 42.4 us -> none  [the longest x1 21.9 us: on_device(): lax.all_to_all(greater, 'energy', split_axis=3, concat_axis=1, tiled=True)]
    all_to_all x1 -> x0, blocking collectives: 29 us -> none  [return_lags(): lax.all_to_all(polarized, 'energy', split_axis=1, concat_axis=2, tiled=True)]
    ppermute x2 -> x0, waiting for transfers between devices: 14.2 us -> none  [the longest x1 9.79 us: with_halo(): lax.ppermute(lax.slice_in_dim(block, block.shape[dim] - width, None, axis...]
    all_to_all x2 -> x0, starting transfers between devices: 11 us -> none  [the longest x1 6.37 us: on_device(): lax.all_to_all(lesser, 'energy', split_axis=2, concat_axis=1, tiled=True)]
    dot_general x20 -> x0, matrix products: 9.44 us -> none  [the longest x2 1.95 us: complex_product(): jnp.einsum('eik,ekj->eij', first_re, second_im, preferred_element_type=jn...]
    ppermute x2 -> x0, starting transfers between devices: 6.86 us -> none  [the longest x1 4.93 us: with_halo(): lax.ppermute(lax.slice_in_dim(block, block.shape[dim] - width, None, axis...]
    unnamed x21 -> x9, local copies, waits for them, and re-layouts: 1.92 us -> 5.64 us
  transfers between devices with their start and end apart: 4 -> 0, of which waited for: 4 -> 0; matrix products, arithmetic and copies ran while one was open for 6% -> 0% of each run, Pallas kernels for 0% -> 0%
where the time goes in v1:
time: 90.1 us; the launch traced here: 89.9 us
  Pallas kernels  84.2 us (93%)
  local copies, waits for them, and re-layouts  5.64 us (6%)
    pallas_call x1, Pallas kernels, fused(): pl.pallas_call(functools.partial(fused_kernel, n, cells), out_shape=jax.S...  84.2 us
    unnamed x9, local copies, waits for them, and re-layouts  5.64 us

profile of v1, /device:TPU:1, one launch (start us, length us, event | category | flops | bytes accessed | tf_op | source)
XLA Modules:
  0.0 89.9 jit_solution(4075907588191709441)
XLA Ops:
  0.0 0.0 copy-start
  0.0 1.2 %copy-done = bf16[1,2,4,256,256]{4,3,2,1,0:T(8,128)(2,1)S(1)} copy-done((bf16[1,2,4,256,256]{4,3,2,1,0:T(8,128)(2,1)S(1)}, bf16[1,2,4,256,256]{4,3,2,1,0:T(8,128)(2,1)}, u32[]{:S(2)}) %copy-start) | copy-done | bytes 1048600
  1.2 0.0 copy-start.1
  1.2 1.2 %copy-done.1 = bf16[1,2,4,256,256]{4,3,2,1,0:T(8,128)(2,1)S(1)} copy-done((bf16[1,2,4,256,256]{4,3,2,1,0:T(8,128)(2,1)S(1)}, bf16[1,2,4,256,256]{4,3,2,1,0:T(8,128)(2,1)}, u32[]{:S(2)}) %copy-start.1) | copy-done | bytes 1048600
  2.5 0.0 copy-start.2
  2.5 1.2 %copy-done.2 = bf16[1,2,4,256,256]{4,3,2,1,0:T(8,128)(2,1)S(1)} copy-done((bf16[1,2,4,256,256]{4,3,2,1,0:T(8,128)(2,1)S(1)}, bf16[1,2,4,256,256]{4,3,2,1,0:T(8,128)(2,1)}, u32[]{:S(2)}) %copy-start.2) | copy-done | bytes 1048600
  3.7 0.0 copy-start.3
  3.7 1.0 %copy-done.3 = bf16[1,3,256,256]{3,2,1,0:T(8,128)(2,1)S(1)} copy-done((bf16[1,3,256,256]{3,2,1,0:T(8,128)(2,1)S(1)}, bf16[1,3,256,256]{3,2,1,0:T(8,128)(2,1)}, u32[]{:S(2)}) %copy-start.3) | copy-done | bytes 393240
  4.7 84.2 %shard_map.46 = bf16[2,4,256,256]{3,2,1,0:T(8,128)(2,1)S(1)} custom-call(bf16[2,4,256,256]{3,2,1,0:T(8,128)(2,1)S(1)} %bitcast.6, bf16[2,4,256,256]{3,2,1,0:T(8,128)(2,1)S(1)} %bitcast.7, bf16[2,4,256,256]{3,2,1,0:T(8,128)(2,1)S(1)} %bitcast.8, bf16[3,256,256]{2,1,0:T(8,128)(2,1)S(1)} %bitcast.9), custom_call_target="tpu_custom_call" | custom-call | tf_op jit(solution)/shard_map/pallas_call | solution.py:218
  88.9 1.0 %copy.6 = bf16[1,2,4,256,256]{4,3,2,1,0:T(8,128)(2,1)} copy(bf16[1,2,4,256,256]{4,3,2,1,0:T(8,128)(2,1)S(1)} %bitcast.5) | data formatting | bytes 2097152
Async XLA Ops:
  0.0 1.2 %copy-start = (bf16[1,2,4,256,256]{4,3,2,1,0:T(8,128)(2,1)S(1)}, bf16[1,2,4,256,256]{4,3,2,1,0:T(8,128)(2,1)}, u32[]{:S(2)}) copy-start(bf16[1,2,4,256,256]{4,3,2,1,0:T(8,128)(2,1)} %param.4) | copy-start | bytes 3145732
  1.2 1.2 %copy-start.1 = (bf16[1,2,4,256,256]{4,3,2,1,0:T(8,128)(2,1)S(1)}, bf16[1,2,4,256,256]{4,3,2,1,0:T(8,128)(2,1)}, u32[]{:S(2)}) copy-start(bf16[1,2,4,256,256]{4,3,2,1,0:T(8,128)(2,1)} %param.5) | copy-start | bytes 3145732
  2.5 1.2 %copy-start.2 = (bf16[1,2,4,256,256]{4,3,2,1,0:T(8,128)(2,1)S(1)}, bf16[1,2,4,256,256]{4,3,2,1,0:T(8,128)(2,1)}, u32[]{:S(2)}) copy-start(bf16[1,2,4,256,256]{4,3,2,1,0:T(8,128)(2,1)} %param.6) | copy-start | bytes 3145732
  3.7 1.0 %copy-start.3 = (bf16[1,3,256,256]{3,2,1,0:T(8,128)(2,1)S(1)}, bf16[1,3,256,256]{3,2,1,0:T(8,128)(2,1)}, u32[]{:S(2)}) copy-start(bf16[1,3,256,256]{3,2,1,0:T(8,128)(2,1)} %param.7) | copy-start | bytes 1179652

commit v2 on v1

--- a/solution.py
+++ b/solution.py
@@ -11,6 +11,8 @@
 MESH = pl.DeviceIdType.MESH
 ROWS = 16
 LANES = 128
+QUARTERS = 4
+DELAY = 4
 F32 = jnp.float32
 BF16 = jnp.bfloat16
 
@@ -25,16 +27,21 @@
 
 def fused_kernel(
     n, cells, green, sig_l, sig_g, coulomb, out,
-    send, recv, send_p, pol, total,
-    send_sem, recv_sem, ret_send_sem, ret_recv_sem, halo_send_sem, halo_recv_sem,
+    send, recv, part, send_p, pol, total,
+    send_sem, recv_sem, relay_send_sem, relay_recv_sem, part_send_sem, part_recv_sem,
+    ret_send_sem, ret_recv_sem, halo_send_sem, halo_recv_sem,
 ):
     me = lax.axis_index("energy")
     cell = lax.axis_index("cell")
     local = green.shape[1]
     norb = green.shape[2]
-    strip = norb // n
-    row_parts, col_parts = strip // ROWS, norb // LANES
-    chunks = row_parts * col_parts
+    width = n // QUARTERS
+    half = 2 * width
+    quarter, place = me // width, lax.rem(me, width)
+    home = jnp.where(me < half, 1, 2)
+    strip = norb // width
+    col_parts = norb // LANES
+    chunks = strip // ROWS * col_parts
     has_low = cell > 0
     has_high = cell < cells - 1
 
@@ -53,7 +60,7 @@
         pl.semaphore_signal(barrier, inc=1, device_id={"cell": cell + 1}, device_id_type=MESH)
 
     def put(value, comp, e):
-        value = value.astype(BF16).reshape(n, strip, norb)
+        value = value.astype(BF16).reshape(width, strip, norb)
         for q in range(chunks):
             r, c = divmod(q, col_parts)
             send[q, :, comp, e] = value[:, r * ROWS:(r + 1) * ROWS, c * LANES:(c + 1) * LANES]
@@ -74,23 +81,42 @@
 
     pl.semaphore_wait(barrier, n - 1 + has_low.astype(jnp.int32) + has_high.astype(jnp.int32))
 
-    def strip_copy(q, slot, peer):
+
+    def strip_copy(q, slot, where):
         return pltpu.make_async_remote_copy(
-            src_ref=send.at[q, peer], dst_ref=recv.at[q, slot],
-            send_sem=send_sem.at[q, peer], recv_sem=recv_sem.at[q, slot],
-            device_id={"energy": peer}, device_id_type=MESH,
+            src_ref=send.at[q, where], dst_ref=recv.at[q, slot],
+            send_sem=send_sem.at[q, where], recv_sem=recv_sem.at[q, slot],
+            device_id={"energy": home * width + where}, device_id_type=MESH,
         )
+
+    def each_target(act):
+        for where in range(width):
+            pl.when(home * width + where != me)(functools.partial(act, where))
 
     @pl.loop(0, chunks)
     def _(q):
-        @pl.loop(1, n)
-        def _(k):
-            strip_copy(q, me, lax.rem(me + k, n)).start()
-
-    @pl.loop(0, chunks)
-    def _(q):
-        recv[q, me] = send[q, me]
-        recv[q, n] = jnp.zeros_like(recv[q, n])
+        each_target(lambda where: strip_copy(q, me, where).start())
+
+    @pl.when(quarter == home)
+    def _():
+        @pl.loop(0, chunks)
+        def _(q):
+            recv[q, me] = send[q, place]
+
+    blank = jnp.zeros((2, local, ROWS, LANES), BF16)
+
+    @pl.when(quarter == 1)
+    def _():
+        @pl.loop(0, chunks)
+        def _(q):
+            recv[q, half, 0:2] = blank
+
+    @pl.when(quarter == 2)
+    def _():
+        @pl.loop(0, chunks)
+        def _(q):
+            recv[q, half - 1, 0:2] = blank
+            recv[q, n, 0:2] = blank
 
     @pl.when(jnp.logical_not(has_low))
     def _():
@@ -100,21 +126,41 @@
     def _():
         pol[2] = jnp.zeros_like(pol[2])
 
-    def window(slot, owner, q):
+    def spot(q):
         rows = pl.ds(pl.multiple_of(q // col_parts * ROWS, ROWS), ROWS)
-        cols = pl.ds(pl.multiple_of(q % col_parts * LANES, LANES), LANES)
-        return pol.at[slot, :, :, owner, rows, cols]
-
-    def return_copy(q, slot, peer):
+        return rows, pl.ds(pl.multiple_of(q % col_parts * LANES, LANES), LANES)
+
+    def relay_copy(q):
         return pltpu.make_async_remote_copy(
-            src_ref=send_p.at[q, peer], dst_ref=window(1, slot, q),
-            send_sem=ret_send_sem.at[q, peer], recv_sem=ret_recv_sem.at[q, slot],
-            device_id={"energy": peer}, device_id_type=MESH,
+            src_ref=recv.at[q, 0:half, 2:4], dst_ref=recv.at[q, 0:half, 2:4],
+            send_sem=relay_send_sem.at[q], recv_sem=relay_recv_sem.at[q],
+            device_id={"energy": 2 * width + place}, device_id_type=MESH,
         )
 
+    def part_copy(q):
+        return pltpu.make_async_remote_copy(
+            src_ref=send_p.at[q, 0:half], dst_ref=part.at[q],
+            send_sem=part_send_sem.at[q], recv_sem=part_recv_sem.at[q],
+            device_id={"energy": width + place}, device_id_type=MESH,
+        )
+
+    def return_copy(q, where, owner):
+        return pltpu.make_async_remote_copy(
+            src_ref=send_p.at[q, owner], dst_ref=pol.at[1, :, :, where, *spot(q)],
+            send_sem=ret_send_sem.at[q, owner], recv_sem=ret_recv_sem.at[q, where],
+            device_id={"energy": owner}, device_id_type=MESH,
+        )
+
+    def halo_copy(q, slot, other):
+        return pltpu.make_async_remote_copy(
+            src_ref=pol.at[1, :, :, :, *spot(q)], dst_ref=pol.at[slot, :, :, :, *spot(q)],
+            send_sem=halo_send_sem.at[q, slot // 2], recv_sem=halo_recv_sem.at[q, slot // 2],
+            device_id={"cell": other}, device_id_type=MESH,
+        )
+
     factor = 1.0 / math.sqrt(n * local)
 
-    def correlate(q, b):
+    def correlate(q, b, first_step, last_step):
         def step(a, acc):
             first = [
                 (recv[q, a + b + i // local, 0, i % local].astype(F32), recv[q, a + b + i // local, 1, i % local].astype(F32))
@@ -130,40 +176,31 @@
             return tuple(acc)
 
         zero = jnp.zeros((ROWS, LANES), F32)
-        acc = lax.fori_loop(0, n - b, step, (zero,) * (2 * local))
-        for w in range(local):
-            send_p[q, b, 0, w] = (acc[2 * w] * factor).astype(BF16)
-            send_p[q, b, 1, w] = (acc[2 * w + 1] * factor).astype(BF16)
-
-    @pl.loop(0, chunks)
-    def _(q):
-        @pl.loop(1, n)
-        def _(k):
-            strip_copy(q, lax.rem(me + k, n), lax.rem(me + k, n)).wait_recv()
-
-        @pl.loop(1, n)
-        def _(k):
-            peer = lax.rem(me + k, n)
-            correlate(q, peer)
-            return_copy(q, me, peer).start()
-
-        correlate(q, me)
-        window(1, me, q)[...] = send_p[q, me]
-
-    def halo_copy(q, slot, other):
-        rows = pl.ds(pl.multiple_of(q // col_parts * ROWS, ROWS), ROWS)
-        cols = pl.ds(pl.multiple_of(q % col_parts * LANES, LANES), LANES)
-        return pltpu.make_async_remote_copy(
-            src_ref=pol.at[1, :, :, :, rows, cols], dst_ref=pol.at[slot, :, :, :, rows, cols],
-            send_sem=halo_send_sem.at[q, slot // 2], recv_sem=halo_recv_sem.at[q, slot // 2],
-            device_id={"cell": other}, device_id_type=MESH,
-        )
-
-    @pl.loop(0, chunks)
-    def _(q):
-        @pl.loop(1, n)
-        def _(k):
-            return_copy(q, lax.rem(me + k, n), lax.rem(me + k, n)).wait_recv()
+        acc = lax.fori_loop(first_step, last_step, step, (zero,) * (2 * local))
+        return [value * factor for value in acc]
+
+    def hand_out(q, owner):
+        @pl.when(owner != me)
+        def _():
+            return_copy(q, place, owner).start()
+
+        @pl.when(owner == me)
+        def _():
+            pol[1, :, :, place, *spot(q)] = send_p[q, owner]
+
+    def gather(q):
+        for slot in range(n):
+            belongs = (quarter == 1) if slot < half else (quarter == 2)
+
+            @pl.when(jnp.logical_and(belongs, me != slot))
+            def _():
+                strip_copy(q, slot, 0).wait_recv()
+
+    def halo(q):
+        for where in range(width):
+            @pl.when(home * width + where != me)
+            def _():
+                return_copy(q, where, 0).wait_recv()
 
         @pl.when(has_low)
         def _():
@@ -172,6 +209,68 @@
         @pl.when(has_high)
         def _():
             halo_copy(q, 0, cell + 1).start()
+
+    @pl.when(quarter == 2)
+    def _():
+        @pl.loop(0, chunks)
+        def _(q):
+            gather(q)
+            relay_copy(q).wait_recv()
+
+            @pl.loop(0, n)
+            def _(b):
+                acc = correlate(q, b, jnp.maximum(half - 1 - b, 0), n - b)
+                for w in range(local):
+                    send_p[q, b, 0, w] = acc[2 * w].astype(BF16)
+                    send_p[q, b, 1, w] = acc[2 * w + 1].astype(BF16)
+
+                @pl.when(b == half)
+                def _():
+                    part_copy(q).start()
+
+                @pl.when(b >= half)
+                def _():
+                    hand_out(q, b)
+
+            @pl.when(q > 0)
+            def _():
+                halo(q - 1)
+
+        halo(chunks - 1)
+
+    delay = min(DELAY, chunks)
+
+    @pl.when(quarter == 1)
+    def _():
+        @pl.loop(0, chunks + delay + 1)
+        def _(t):
+            @pl.when(t < chunks)
+            def _():
+                gather(t)
+                relay_copy(t).start()
+
+            @pl.when(jnp.logical_and(t >= delay, t < chunks + delay))
+            def _():
+                q = t - delay
+                part_copy(q).wait_recv()
+
+                @pl.loop(0, half)
+                def _(b):
+                    acc = correlate(q, b, 0, half - b)
+                    for w in range(local):
+                        send_p[q, b, 0, w] = (acc[2 * w] + part[q, b, 0, w].astype(F32)).astype(BF16)
+                        send_p[q, b, 1, w] = (acc[2 * w + 1] + part[q, b, 1, w].astype(F32)).astype(BF16)
+                    hand_out(q, b)
+
+            @pl.when(t > delay)
+            def _():
+                halo(t - delay - 1)
+
+    @pl.when(quarter != home)
+    def _():
+        @pl.loop(0, chunks)
+        def _(q):
+            halo(q)
 
     def polarized(slot, c, e):
         return pol[slot, c, e].reshape(norb, norb)
@@ -201,17 +300,33 @@
 
     @pl.loop(0, chunks)
     def _(q):
-        @pl.loop(1, n)
-        def _(k):
-            peer = lax.rem(me + k, n)
-            strip_copy(q, me, peer).wait_send()
-            return_copy(q, me, peer).wait_send()
+        each_target(lambda where: strip_copy(q, me, where).wait_send())
+
+        @pl.when(quarter == 1)
+        def _():
+            relay_copy(q).wait_send()
+
+        @pl.when(quarter == 2)
+        def _():
+            part_copy(q).wait_send()
+
+        @pl.when(quarter == home)
+        def _():
+            @pl.loop(0, half)
+            def _(b):
+                owner = (home - 1) * half + b
+
+                @pl.when(owner != me)
+                def _():
+                    return_copy(q, place, owner).wait_send()
 
 
 def fused(n, cells, retarded, sigma_lesser, sigma_greater, coulomb):
     green = retarded[0]
     local, norb = green.shape[1], green.shape[2]
-    strip = norb // n
+    width = n // QUARTERS
+    half = 2 * width
+    strip = norb // width
     chunks = strip // ROWS * (norb // LANES)
     vmem = pl.BlockSpec(memory_space=pltpu.VMEM)
     dma = pltpu.SemaphoreType.DMA
@@ -221,16 +336,19 @@
         in_specs=[vmem] * 4,
         out_specs=vmem,
         scratch_shapes=[
-            pltpu.VMEM((chunks, n, 4, local, ROWS, LANES), BF16),
+            pltpu.VMEM((chunks, width, 4, local, ROWS, LANES), BF16),
             pltpu.VMEM((chunks, n + 1, 4, local, ROWS, LANES), BF16),
+            pltpu.VMEM((chunks, half, 2, local, ROWS, LANES), BF16),
             pltpu.VMEM((chunks, n, 2, local, ROWS, LANES), BF16),
-            pltpu.VMEM((3, 2, local, n, strip, norb), BF16),
+            pltpu.VMEM((3, 2, local, width, strip, norb), BF16),
             pltpu.VMEM((2, local, norb, norb), F32),
-            dma((chunks, n)), dma((chunks, n)), dma((chunks, n)), dma((chunks, n)),
+            dma((chunks, width)), dma((chunks, n)),
+            dma((chunks,)), dma((chunks,)), dma((chunks,)), dma((chunks,)),
+            dma((chunks, n)), dma((chunks, width)),
             dma((chunks, 2)), dma((chunks, 2)),
         ],
         compiler_params=pltpu.CompilerParams(
-            collective_id=0, has_side_effects=True, vmem_limit_bytes=48 * 1024 * 1024
+            collective_id=0, has_side_effects=True, vmem_limit_bytes=56 * 1024 * 1024
         ),
     )(green, sigma_lesser[0], sigma_greater[0], coulomb[0])
     return result[None]
@@ -281,7 +399,7 @@
 
     def on_device(retarded, sigma_lesser, sigma_greater, coulomb):
         norb = retarded.shape[-1]
-        whole_tiles = norb % LANES == 0 and norb % (n * ROWS) == 0
+        whole_tiles = n % QUARTERS == 0 and norb % LANES == 0 and norb % (n // QUARTERS * ROWS) == 0
         plan = fused if whole_tiles else thin
         return plan(n, cells, retarded, sigma_lesser, sigma_greater, coulomb)
 

time: 90.1 us -> 114 us (1.27)
  Pallas kernels: 84.2 us -> 112 us
  local copies, waits for them, and re-layouts: 5.64 us -> 2.26 us
    pallas_call x1, Pallas kernels: 84.2 us -> 112 us  [fused(): pl.pallas_call(functools.partial(fused_kernel, n, cells), out_shape=jax.S...]
    unnamed x9 -> x1, local copies, waits for them, and re-layouts: 5.64 us -> 2.26 us
where the time goes in v2:
time: 114 us
  Pallas kernels  112 us (98%)
  local copies, waits for them, and re-layouts  2.26 us (2%)
    pallas_call x1, Pallas kernels, fused(): pl.pallas_call(functools.partial(fused_kernel, n, cells), out_shape=jax.S...  112 us

profile of v2, /device:TPU:1, one launch (start us, length us, event | category | flops | bytes accessed | tf_op | source)
XLA Modules:
  0.0 114.0 jit_solution(11575403869926757788)
XLA Ops:
  0.0 111.7 %shard_map.46 = bf16[2,4,256,256]{3,2,1,0:T(8,128)(2,1)} custom-call(bf16[2,4,256,256]{3,2,1,0:T(8,128)(2,1)} %bitcast.6, bf16[2,4,256,256]{3,2,1,0:T(8,128)(2,1)} %bitcast.7, bf16[2,4,256,256]{3,2,1,0:T(8,128)(2,1)} %bitcast.8, bf16[3,256,256]{2,1,0:T(8,128)(2,1)} %bitcast.9), custom_call_target="tpu_custom_call" | custom-call | tf_op jit(solution)/shard_map/pallas_call | solution.py:333
  111.7 2.3 %copy.6 = bf16[1,2,4,256,256]{4,3,2,1,0:T(8,128)(2,1)} copy(bf16[1,2,4,256,256]{4,3,2,1,0:T(8,128)(2,1)} %bitcast.5) | data formatting | bytes 2097152

commit v3 on v2

--- a/solution.py
+++ b/solution.py
@@ -12,7 +12,9 @@
 ROWS = 16
 LANES = 128
 QUARTERS = 4
-DELAY = 4
+DELAY = 6
+LATE = 4
+LEAD = 3
 F32 = jnp.float32
 BF16 = jnp.bfloat16
 
@@ -26,9 +28,9 @@
 
 
 def fused_kernel(
-    n, cells, green, sig_l, sig_g, coulomb, out,
-    send, recv, part, send_p, pol, total,
-    send_sem, recv_sem, relay_send_sem, relay_recv_sem, part_send_sem, part_recv_sem,
+    n, cells, green_in, sig_l_in, sig_g_in, coulomb_in, out,
+    green, sig_l, sig_g, coulomb, in_sem, coulomb_sem, send, recv, part, send_p, pol, total,
+    send_sem, recv_sem, forward_send_sem, forward_recv_sem, relay_send_sem, relay_recv_sem, part_send_sem, part_recv_sem,
     ret_send_sem, ret_recv_sem, halo_send_sem, halo_recv_sem,
 ):
     me = lax.axis_index("energy")
@@ -45,6 +47,18 @@
     has_low = cell > 0
     has_high = cell < cells - 1
 
+    def loads(e):
+        return [
+            pltpu.make_async_copy(source.at[:, e], held.at[:, e], in_sem.at[i, e])
+            for i, (source, held) in enumerate(((green_in, green), (sig_l_in, sig_l), (sig_g_in, sig_g)))
+        ]
+
+    for e in range(local):
+        for load in loads(e):
+            load.start()
+    coulomb_load = pltpu.make_async_copy(coulomb_in, coulomb, coulomb_sem)
+    coulomb_load.start()
+
     barrier = pltpu.get_barrier_semaphore()
 
     @pl.loop(1, n)
@@ -67,6 +81,8 @@
 
     @pl.loop(0, local)
     def _(e):
+        for load in loads(e):
+            load.wait()
         g_re, g_im = green[0, e], green[1, e]
         l_re, l_im = sig_l[0, e], sig_l[1, e]
         half_re = (nn(g_re, l_re) - nn(g_im, l_im)).astype(BF16)
@@ -86,22 +102,27 @@
         return pltpu.make_async_remote_copy(
             src_ref=send.at[q, where], dst_ref=recv.at[q, slot],
             send_sem=send_sem.at[q, where], recv_sem=recv_sem.at[q, slot],
-            device_id={"energy": home * width + where}, device_id_type=MESH,
+            device_id={"energy": quarter * width + where}, device_id_type=MESH,
         )
 
     def each_target(act):
         for where in range(width):
-            pl.when(home * width + where != me)(functools.partial(act, where))
+            pl.when(where != place)(functools.partial(act, where))
+
+    lead = jnp.where(quarter == home, min(LEAD, chunks), chunks)
+
+    @pl.loop(0, lead)
+    def _(q):
+        each_target(lambda where: strip_copy(q, me, where).start())
+
+    def more(q):
+        @pl.when(q + lead < chunks)
+        def _():
+            each_target(lambda where: strip_copy(q + lead, me, where).start())
 
     @pl.loop(0, chunks)
     def _(q):
-        each_target(lambda where: strip_copy(q, me, where).start())
-
-    @pl.when(quarter == home)
-    def _():
-        @pl.loop(0, chunks)
-        def _(q):
-            recv[q, me] = send[q, place]
+        recv[q, me] = send[q, place]
 
     blank = jnp.zeros((2, local, ROWS, LANES), BF16)
 
@@ -129,6 +150,14 @@
     def spot(q):
         rows = pl.ds(pl.multiple_of(q // col_parts * ROWS, ROWS), ROWS)
         return rows, pl.ds(pl.multiple_of(q % col_parts * LANES, LANES), LANES)
+
+    def forward_copy(q, kind):
+        block = (q, pl.ds(quarter * width, width), slice(2 * kind, 2 * kind + 2))
+        return pltpu.make_async_remote_copy(
+            src_ref=recv.at[block], dst_ref=recv.at[block],
+            send_sem=forward_send_sem.at[q, kind], recv_sem=forward_recv_sem.at[q, kind],
+            device_id={"energy": home * width + place}, device_id_type=MESH,
+        )
 
     def relay_copy(q):
         return pltpu.make_async_remote_copy(
@@ -189,12 +218,7 @@
             pol[1, :, :, place, *spot(q)] = send_p[q, owner]
 
     def gather(q):
-        for slot in range(n):
-            belongs = (quarter == 1) if slot < half else (quarter == 2)
-
-            @pl.when(jnp.logical_and(belongs, me != slot))
-            def _():
-                strip_copy(q, slot, 0).wait_recv()
+        each_target(lambda where: strip_copy(q, quarter * width + where, where).wait_recv())
 
     def halo(q):
         for where in range(width):
@@ -215,6 +239,9 @@
         @pl.loop(0, chunks)
         def _(q):
             gather(q)
+            more(q)
+            forward_copy(q, 1).wait_recv()
+            forward_copy(q, 0).wait_recv()
             relay_copy(q).wait_recv()
 
             @pl.loop(0, n)
@@ -232,26 +259,30 @@
                 def _():
                     hand_out(q, b)
 
-            @pl.when(q > 0)
+            @pl.when(q >= LATE)
             def _():
-                halo(q - 1)
-
-        halo(chunks - 1)
+                halo(q - LATE)
+
+        for q in range(max(chunks - LATE, 0), chunks):
+            halo(q)
 
     delay = min(DELAY, chunks)
 
     @pl.when(quarter == 1)
     def _():
-        @pl.loop(0, chunks + delay + 1)
+        @pl.loop(0, chunks + delay + LATE)
         def _(t):
             @pl.when(t < chunks)
             def _():
                 gather(t)
+                forward_copy(t, 1).wait_recv()
                 relay_copy(t).start()
+                more(t)
 
             @pl.when(jnp.logical_and(t >= delay, t < chunks + delay))
             def _():
                 q = t - delay
+                forward_copy(q, 0).wait_recv()
                 part_copy(q).wait_recv()
 
                 @pl.loop(0, half)
@@ -262,18 +293,26 @@
                         send_p[q, b, 1, w] = (acc[2 * w + 1] + part[q, b, 1, w].astype(F32)).astype(BF16)
                     hand_out(q, b)
 
-            @pl.when(t > delay)
+            @pl.when(t >= delay + LATE)
             def _():
-                halo(t - delay - 1)
+                halo(t - delay - LATE)
 
     @pl.when(quarter != home)
     def _():
+        @pl.loop(0, chunks)
+        def _(q):
+            gather(q)
+            forward_copy(q, 1).start()
+            forward_copy(q, 0).start()
+
         @pl.loop(0, chunks)
         def _(q):
             halo(q)
 
     def polarized(slot, c, e):
         return pol[slot, c, e].reshape(norb, norb)
+
+    coulomb_load.wait()
 
     @pl.loop(0, local)
     def _(e):
@@ -301,6 +340,11 @@
     @pl.loop(0, chunks)
     def _(q):
         each_target(lambda where: strip_copy(q, me, where).wait_send())
+
+        @pl.when(quarter != home)
+        def _():
+            forward_copy(q, 1).wait_send()
+            forward_copy(q, 0).wait_send()
 
         @pl.when(quarter == 1)
         def _():
@@ -333,16 +377,21 @@
     result = pl.pallas_call(
         functools.partial(fused_kernel, n, cells),
         out_shape=jax.ShapeDtypeStruct(green.shape, BF16),
-        in_specs=[vmem] * 4,
+        in_specs=[pl.BlockSpec(memory_space=pltpu.HBM)] * 4,
         out_specs=vmem,
         scratch_shapes=[
+            pltpu.VMEM(green.shape, BF16),
+            pltpu.VMEM(green.shape, BF16),
+            pltpu.VMEM(green.shape, BF16),
+            pltpu.VMEM(coulomb.shape[1:], BF16),
+            dma((3, local)), dma,
             pltpu.VMEM((chunks, width, 4, local, ROWS, LANES), BF16),
             pltpu.VMEM((chunks, n + 1, 4, local, ROWS, LANES), BF16),
             pltpu.VMEM((chunks, half, 2, local, ROWS, LANES), BF16),
             pltpu.VMEM((chunks, n, 2, local, ROWS, LANES), BF16),
             pltpu.VMEM((3, 2, local, width, strip, norb), BF16),
             pltpu.VMEM((2, local, norb, norb), F32),
-            dma((chunks, width)), dma((chunks, n)),
+            dma((chunks, width)), dma((chunks, n)), dma((chunks, 2)), dma((chunks, 2)),
             dma((chunks,)), dma((chunks,)), dma((chunks,)), dma((chunks,)),
             dma((chunks, n)), dma((chunks, width)),
             dma((chunks, 2)), dma((chunks, 2)),

time: 114 us -> 81.9 us (0.72)
  Pallas kernels: 112 us -> 79.5 us
    pallas_call x1, Pallas kernels: 112 us -> 79.5 us  [fused(): pl.pallas_call(functools.partial(fused_kernel, n, cells), out_shape=jax.S...]
where the time goes in v3:
time: 81.9 us; the launch traced here: 81.7 us
  Pallas kernels  79.5 us (97%)
  local copies, waits for them, and re-layouts  2.26 us (3%)
    pallas_call x1, Pallas kernels, fused(): pl.pallas_call(functools.partial(fused_kernel, n, cells), out_shape=jax.S...  79.5 us
    unnamed x1, local copies, waits for them, and re-layouts  2.26 us

profile of v3, /device:TPU:1, one launch (start us, length us, event | category | flops | bytes accessed | tf_op | source)
XLA Modules:
  0.0 81.7 jit_solution(16370325333171870444)
XLA Ops:
  0.0 79.5 %shard_map.46 = bf16[2,4,256,256]{3,2,1,0:T(8,128)(2,1)} custom-call(bf16[2,4,256,256]{3,2,1,0:T(8,128)(2,1)} %bitcast.6, bf16[2,4,256,256]{3,2,1,0:T(8,128)(2,1)} %bitcast.7, bf16[2,4,256,256]{3,2,1,0:T(8,128)(2,1)} %bitcast.8, bf16[3,256,256]{2,1,0:T(8,128)(2,1)} %bitcast.9), custom_call_target="tpu_custom_call" | custom-call | tf_op jit(solution)/shard_map/pallas_call | solution.py:377
  79.5 2.3 %copy.6 = bf16[1,2,4,256,256]{4,3,2,1,0:T(8,128)(2,1)} copy(bf16[1,2,4,256,256]{4,3,2,1,0:T(8,128)(2,1)} %bitcast.5) | data formatting | bytes 2097152

commit v4 on v3

--- a/solution.py
+++ b/solution.py
@@ -14,6 +14,8 @@
 QUARTERS = 4
 DELAY = 6
 LATE = 4
+LAG = 0
+SHIFT = 4
 LEAD = 3
 F32 = jnp.float32
 BF16 = jnp.bfloat16
@@ -159,10 +161,11 @@
             device_id={"energy": home * width + place}, device_id_type=MESH,
         )
 
-    def relay_copy(q):
-        return pltpu.make_async_remote_copy(
-            src_ref=recv.at[q, 0:half, 2:4], dst_ref=recv.at[q, 0:half, 2:4],
-            send_sem=relay_send_sem.at[q], recv_sem=relay_recv_sem.at[q],
+    def relay_copy(q, origin):
+        block = (q, slice(origin * width, (origin + 1) * width), slice(2, 4))
+        return pltpu.make_async_remote_copy(
+            src_ref=recv.at[block], dst_ref=recv.at[block],
+            send_sem=relay_send_sem.at[q, origin], recv_sem=relay_recv_sem.at[q, origin],
             device_id={"energy": 2 * width + place}, device_id_type=MESH,
         )
 
@@ -242,7 +245,8 @@
             more(q)
             forward_copy(q, 1).wait_recv()
             forward_copy(q, 0).wait_recv()
-            relay_copy(q).wait_recv()
+            relay_copy(q, 1).wait_recv()
+            relay_copy(q, 0).wait_recv()
 
             @pl.loop(0, n)
             def _(b):
@@ -267,6 +271,7 @@
             halo(q)
 
     delay = min(DELAY, chunks)
+    lag = min(LAG, delay)
 
     @pl.when(quarter == 1)
     def _():
@@ -275,9 +280,13 @@
             @pl.when(t < chunks)
             def _():
                 gather(t)
-                forward_copy(t, 1).wait_recv()
-                relay_copy(t).start()
+                relay_copy(t, 1).start()
                 more(t)
+
+            @pl.when(jnp.logical_and(t >= lag, t < chunks + lag))
+            def _():
+                forward_copy(t - lag, 1).wait_recv()
+                relay_copy(t - lag, 0).start()
 
             @pl.when(jnp.logical_and(t >= delay, t < chunks + delay))
             def _():
@@ -299,11 +308,18 @@
 
     @pl.when(quarter != home)
     def _():
-        @pl.loop(0, chunks)
+        shift = jnp.where(quarter == 0, min(SHIFT, chunks), 0)
+
+        @pl.loop(0, chunks + shift)
         def _(q):
-            gather(q)
-            forward_copy(q, 1).start()
-            forward_copy(q, 0).start()
+            @pl.when(q < chunks)
+            def _():
+                gather(q)
+                forward_copy(q, 1).start()
+
+            @pl.when(q >= shift)
+            def _():
+                forward_copy(q - shift, 0).start()
 
         @pl.loop(0, chunks)
         def _(q):
@@ -348,7 +364,8 @@
 
         @pl.when(quarter == 1)
         def _():
-            relay_copy(q).wait_send()
+            relay_copy(q, 0).wait_send()
+            relay_copy(q, 1).wait_send()
 
         @pl.when(quarter == 2)
         def _():
@@ -392,7 +409,7 @@
             pltpu.VMEM((3, 2, local, width, strip, norb), BF16),
             pltpu.VMEM((2, local, norb, norb), F32),
             dma((chunks, width)), dma((chunks, n)), dma((chunks, 2)), dma((chunks, 2)),
-            dma((chunks,)), dma((chunks,)), dma((chunks,)), dma((chunks,)),
+            dma((chunks, 2)), dma((chunks, 2)), dma((chunks,)), dma((chunks,)),
             dma((chunks, n)), dma((chunks, width)),
             dma((chunks, 2)), dma((chunks, 2)),
         ],

time: 81.9 us -> 80.7 us (0.985)
  Pallas kernels: 79.5 us -> 78.3 us
    pallas_call x1, Pallas kernels: 79.5 us -> 78.3 us  [fused(): pl.pallas_call(functools.partial(fused_kernel, n, cells), out_shape=jax.S...]
where the time goes in v4:
time: 80.7 us; the launch traced here: 80.6 us
  Pallas kernels  78.3 us (97%)
  local copies, waits for them, and re-layouts  2.26 us (3%)
    pallas_call x1, Pallas kernels, fused(): pl.pallas_call(functools.partial(fused_kernel, n, cells), out_shape=jax.S...  78.3 us
    unnamed x1, local copies, waits for them, and re-layouts  2.26 us

profile of v4, /device:TPU:1, one launch (start us, length us, event | category | flops | bytes accessed | tf_op | source)
XLA Modules:
  0.0 80.6 jit_solution(3175387292632839149)
XLA Ops:
  0.0 78.3 %shard_map.46 = bf16[2,4,256,256]{3,2,1,0:T(8,128)(2,1)} custom-call(bf16[2,4,256,256]{3,2,1,0:T(8,128)(2,1)} %bitcast.6, bf16[2,4,256,256]{3,2,1,0:T(8,128)(2,1)} %bitcast.7, bf16[2,4,256,256]{3,2,1,0:T(8,128)(2,1)} %bitcast.8, bf16[3,256,256]{2,1,0:T(8,128)(2,1)} %bitcast.9), custom_call_target="tpu_custom_call" | custom-call | tf_op jit(solution)/shard_map/pallas_call | solution.py:394
  78.3 2.3 %copy.6 = bf16[1,2,4,256,256]{4,3,2,1,0:T(8,128)(2,1)} copy(bf16[1,2,4,256,256]{4,3,2,1,0:T(8,128)(2,1)} %bitcast.5) | data formatting | bytes 2097152
